TPU v7x, 256 devices: a whole 4x4x8 slice. The times are simulated.
256 devices in a mesh: lon: 64 (over x_hi, z, y), lat: 4 (over x_lo, core).
Axes of the slice: x: 4 (x_hi: 2, x_lo: 2; x = x_hi * 2 + x_lo), y: 4, z: 8, core: 2. Of those that a mesh axis runs over, the one named last changes fastest.
Arguments:
- inputs: bfloat16 [32, 8192, 512], P('lat', 'lon'), may hold values from -16 to 16
- d_out: bfloat16 [32, 8192, 512], P('lat', 'lon'), may hold values from -6 to 6
- w_qkv: bfloat16 [512, 1536], replicated, may hold values from -0.25 to 0.25
- w_proj: bfloat16 [512, 512], replicated, may hold values from -0.25 to 0.25
- gain: float32 [512], replicated, may hold values from 0.1 to 1.9
- bias_table: float32 [465, 16], replicated, may hold values from -400 to 400
- rel_index: int32 [128, 128], replicated, may hold values from 0 to 464, as said below
- shifts: int32 [4], P('lat'), may hold values from 1 to 15, as said below
Outputs:
- d_inputs: bfloat16 [32, 8192, 512], P('lat', 'lon')
- g_qkv: float32 [512, 1536], P(('lon', 'lat'))
- g_proj: float32 [512, 512], P(('lon', 'lat'))
- g_gain: float32 [512], P(('lon', 'lat'))
- g_table: float32 [465, 16], replicated
Inputs may be any that keep to these rules, and one draw needn't show every extreme that they name: `rel_index`: entry (i, j) depends only on the row and column offsets between window positions i and j, and distinct offsets give distinct entries. `shifts`: some band is shifted by 16 - 1.
All inputs are finite; a program needn't handle non-finite values.
Results may differ from a plain program's by a relative error of at most 0.0095.
Values may be sent and summed in bfloat16 or wider, within the bound.
A program may use at most 128 MiB of HBM per device.

v0:
```python
import functools

import jax
import jax.numpy as jnp
from jax import lax
from jax.experimental import pallas as pl
from jax.experimental.pallas import tpu as pltpu
from jax.sharding import PartitionSpec as P

C = 512
H = 16
HD = 32
WH = 8
WW = 16
WIN = 128
NREL = 465
COLS = 128
NWIN = 8
GROUPS = 4
TOK = NWIN * WIN
EPSILON = 1e-05
LOG2E = 1.4426950408889634
F32 = jnp.float32
BF16 = jnp.bfloat16

NN = (((1,), (0,)), ((), ()))
NT = (((1,), (1,)), ((), ()))


def mm(a, b, dims=NN):
    return lax.dot_general(a, b, dims, preferred_element_type=F32)


def iota(shape, dim):
    return lax.broadcasted_iota(jnp.int32, shape, dim)


def one_hot(cond):
    return jnp.where(cond, 1.0, 0.0).astype(BF16)


def split3(x):
    hi = x.astype(BF16)
    rest = x - hi.astype(F32)
    mid = rest.astype(BF16)
    low = (rest - mid.astype(F32)).astype(BF16)
    return hi, mid, low


def pair_masks(j):
    k = iota((WIN, WIN), 1)
    carry = (j % WW + k % WW) >= WW
    wrap = (j // WW + k // WW + carry.astype(jnp.int32)) >= WH
    return carry, wrap


def head_masks(rows):
    lane = iota((rows, 128), 1)
    return [(lane // HD) == h for h in range(4)]


NX, NY, NZ = 4, 4, 8
PIECES = (C, 384, 384, 384, 384)
X_FIRST = (True, False, True, False, True)


class Place:
    def __init__(self):
        lon = lax.axis_index("lon")
        lat = lax.axis_index("lat")
        self.lon, self.lat = lon, lat
        self.core = lax.rem(lat, 2)
        self.x = (lon // 32) * 2 + lat // 2
        self.z = lax.rem(lon // 4, 8)
        self.y = lax.rem(lon, 4)

    def at(self, x=None, y=None, z=None, core=None):
        x = self.x if x is None else x
        y = self.y if y is None else y
        z = self.z if z is None else z
        core = self.core if core is None else core
        return ((x // 2) * 32 + z * 4 + y, lax.rem(x, 2) * 2 + core)

    def partner(self):
        return self.at(core=1 - self.core)

    def along(self, axis, step):
        if axis == "core":
            return self.partner()
        if axis == "x":
            return self.at(x=lax.rem(self.x + step, NX))
        if axis == "y":
            return self.at(y=lax.rem(self.y + step, NY))
        return self.at(z=lax.rem(self.z + step, NZ))

    def slab(self, step):
        return (lax.rem(self.lon + 64 + step, 64), self.lat)


def remote(src, dst, send, recv, device):
    return pltpu.make_async_remote_copy(
        src_ref=src, dst_ref=dst, send_sem=send, recv_sem=recv,
        device_id=device, device_id_type=pl.DeviceIdType.MESH,
    )


class Reduction:
    def __init__(self, here, refs, x_first, table):
        self.here = here
        (self.s0, self.r0, self.s1, self.r1, self.s2, self.r2, self.s3, self.r3,
         self.send, self.recv) = refs
        self.axes = ("core", "x", "y", "z") if x_first else ("core", "y", "x", "z")
        self.counts = (2, 4, 4, NZ)
        self.table = table

    def copies(self, stage):
        here = self.here
        axis = self.axes[stage]
        out = []
        for step in range(1, self.counts[stage]):
            target = lax.rem(getattr(here, axis) + step, self.counts[stage])
            if stage == 0:
                src, dst = self.s0.at[target], self.r0
            elif stage == 1:
                src = self.s1.at[target] if axis == "x" else self.s1.at[:, target]
                dst = self.r1.at[step - 1]
            elif stage == 2:
                src, dst = self.s2.at[target], self.r2.at[step - 1]
            else:
                src, dst = self.s3.at[target], self.r3.at[step - 1]
            slot = (0, 1, 4, 7)[stage] + step - 1
            out.append(
                remote(src, dst, self.send.at[slot], self.recv.at[slot], here.along(axis, step))
            )
        return out

    def table_copies(self, stage, arriving):
        if self.table is None:
            return []
        slots, send, recv = (part[stage] for part in self.table)
        axis = self.axes[stage]
        me = getattr(self.here, axis)
        out = []
        for step in range(1, self.counts[stage]):
            n = lax.rem(me + step, self.counts[stage]) if arriving else me
            out.append(
                remote(slots.at[me], slots.at[n], send.at[step], recv.at[n], self.here.along(axis, step))
            )
        return out

    def send_off(self, stage, table_value):
        for copy in self.copies(stage):
            copy.start()
        if self.table is not None:
            self.table[0][stage][getattr(self.here, self.axes[stage])] = table_value
            for copy in self.table_copies(stage, False):
                copy.start()

    def arrived(self, stage):
        for copy in self.copies(stage):
            copy.wait_recv()
        for copy in self.table_copies(stage, True):
            copy.wait_recv()
        if self.table is None:
            return None
        slots = self.table[0][stage]
        total = slots[0]
        for n in range(1, self.counts[stage]):
            total = total + slots[n]
        return total

    def start(self, table_value=None):
        self.send_off(0, table_value)

    def step1(self):
        table_value = self.arrived(0)
        for n in range(NX):
            own = self.s0[self.here.core, n].astype(F32)
            self.s1[n] = (own + self.r0[n].astype(F32)).astype(BF16)
        self.send_off(1, table_value)

    def step2(self):
        table_value = self.arrived(1)
        for n in range(4):
            own = self.s1[self.here.x, n] if self.axes[1] == "x" else self.s1[n, self.here.y]
            total = own.astype(F32)
            for r in range(3):
                total = total + self.r1[r, n].astype(F32)
            self.s2[n] = total.astype(BF16)
        self.send_off(2, table_value)

    def step3(self):
        table_value = self.arrived(2)
        total = self.s2[getattr(self.here, self.axes[2])].astype(F32)
        for r in range(3):
            total = total + self.r2[r].astype(F32)
        for z in range(NZ):
            self.s3[z] = total[2 * z:2 * z + 2]
        self.send_off(3, table_value)

    def step4(self):
        table_value = self.arrived(3)
        total = self.s3[self.here.z]
        for r in range(NZ - 1):
            total = total + self.r3[r]
        return total, table_value

    def finish(self):
        for stage in range(4):
            for copy in self.copies(stage) + self.table_copies(stage, False):
                copy.wait_send()


def body(
    n_dev,
    shift_ref, x_ref, d_ref, wqkv_ref, wproj_ref, gain_ref, table_ref, rel_ref,
    out_ref, gq_ref, gp_ref, gg_ref, gt_ref,
    xw, dw, nx, istd, normed, normed_t, qkv, dh, soft, att_t, dproj, dnorm, dsum, bias, hot, g4, ow, att_p,
    tx_ref, td_ref, back_ref, halo_send, halo_recv, *rest,
):
    here = Place()
    peers = [here.partner(), here.slab(1), here.slab(-1)]
    peers += [here.along("x", n) for n in range(1, NX)]
    peers += [here.along("y", n) for n in range(1, NY)]
    peers += [here.along("z", n) for n in range(1, NZ)]
    barrier = pltpu.get_barrier_semaphore()
    for peer in peers:
        pl.semaphore_signal(barrier, inc=1, device_id=peer, device_id_type=pl.DeviceIdType.MESH)
    pl.semaphore_wait(barrier, len(peers))

    edge = pl.ds(COLS - WW, WW)
    halo = [
        remote(src.at[:, edge, :], dst, halo_send.at[n], halo_recv.at[n], here.slab(1))
        for n, (src, dst) in enumerate(((x_ref, tx_ref), (d_ref, td_ref)))
    ]
    for copy in halo:
        copy.start()

    pieces = []
    for p in range(len(PIECES)):
        refs = rest[p * 10:(p + 1) * 10]
        table = None
        if p:
            base = len(PIECES) * 10 + (p - 1) * 12
            table = (rest[base:base + 4], rest[base + 4:base + 8], rest[base + 8:base + 12])
        pieces.append(Reduction(here, refs, X_FIRST[p], table))

    s = shift_ref[0]
    w_i = iota((128, 128), 0)
    c_i = iota((128, 128), 1)
    to_win = one_hot(c_i == w_i - s)
    t_w = iota((16, 16), 0)
    t_c = iota((16, 16), 1)
    tail_win = one_hot(t_c == t_w - s + 16)
    gain = gain_ref[...]
    grad_scale = (TOK * n_dev) ** (-0.5)

    def shift_row(r, _):
        rows = pl.ds(pl.multiple_of(r * WW, WW), WW)
        for src, dst in ((x_ref, xw), (d_ref, dw)):
            y = mm(to_win, src[r]).astype(BF16)
            for w in range(NWIN):
                dst[w, rows, :] = y[w * WW:(w + 1) * WW]
        return 0

    lax.fori_loop(0, WH, shift_row, 0)

    rel_t = rel_ref[...].astype(F32).T
    code_rows = []
    for wrap in (0, 1):
        for carry in (0, 1):
            j = 112 * wrap + 15 * carry
            row = rel_t[j:j + 1, :]
            code_rows.append(pltpu.roll(jnp.broadcast_to(row, (8, 128)), (128 - j) % 128, 1)[0:1])
    code = jnp.concatenate(code_rows, axis=1).astype(jnp.int32)
    hot[...] = one_hot(iota((512, 512), 0) == code)
    tab = jnp.concatenate([table_ref[...], jnp.zeros((512 - NREL, H), F32)], axis=0).T
    tab = tab * LOG2E
    parts = split3(tab)
    t4 = mm(parts[0], hot[...]) + mm(parts[1], hot[...]) + mm(parts[2], hot[...])
    g4[...] = t4
    carry_m, wrap_m = pair_masks(w_i)
    carry_r, wrap_r = pair_masks(127 - w_i)
    reverse = one_hot(w_i + c_i == 127)

    for h in range(H):
        row = [jnp.broadcast_to(g4[h:h + 1, q * 128:(q + 1) * 128], (128, 128)) for q in range(4)]
        base = jnp.where(
            wrap_m, jnp.where(carry_m, row[3], row[2]), jnp.where(carry_m, row[1], row[0])
        )
        bias[h] = pltpu.roll(base, 0, 1, stride=1, stride_axis=0)

    def norm_win(w, _):
        src = xw[w].astype(F32)
        mean = jnp.mean(src, axis=-1, keepdims=True)
        cen = src - mean
        inv = lax.rsqrt(jnp.mean(cen * cen, axis=-1, keepdims=True) + EPSILON)
        n = cen * inv
        nx[w] = n
        istd[w] = inv
        normed[w] = (n * gain).astype(BF16)
        return 0

    lax.fori_loop(1, NWIN, norm_win, 0)

    row_p = iota((C, C), 0)
    p_core, p_x, p_y = row_p // 256, (row_p // 64) % 4, (row_p // 16) % 4
    p_z, p_t = (row_p // 2) % 8, row_p % 2
    source = (p_x // 2) * 256 + p_z * 32 + p_y * 8 + (p_x % 2) * 4 + p_core * 2 + p_t
    order = one_hot(iota((C, C), 1) == source)

    def project(m, _):
        lhs = normed[pl.ds(2 * m, 2)].reshape(256, C)
        for n in range(3):
            y = mm(lhs, wqkv_ref[:, n * C:(n + 1) * C]).astype(BF16)
            for b in range(4):
                for ww in range(2):
                    qkv[n * 4 + b, 2 * m + ww] = y[ww * 128:(ww + 1) * 128, b * 128:(b + 1) * 128]
        y = mm(dw[pl.ds(2 * m, 2)].reshape(256, C), wproj_ref[...], NT).astype(BF16)
        for b in range(4):
            for ww in range(2):
                dh[b, 2 * m + ww] = y[ww * 128:(ww + 1) * 128, b * 128:(b + 1) * 128]
        normed_t[:, pl.ds(pl.multiple_of(m * 256, 256), 256)] = mm(order, lhs, NT).astype(BF16)
        return 0

    lax.fori_loop(1, 4, project, 0)
    for copy in halo:
        copy.wait_recv()

    def tail_row(r, _):
        rows = pl.ds(pl.multiple_of(r * WW, WW), WW)
        for src, dst in ((tx_ref, xw), (td_ref, dw)):
            y = mm(tail_win, src[r]).astype(BF16)
            dst[0, rows, :] = dst[0, rows, :] + y
        return 0

    lax.fori_loop(0, WH, tail_row, 0)
    norm_win(0, 0)
    project(0, 0)

    masks = head_masks(128)

    def stack_heads(block):
        zero = jnp.zeros_like(block)
        return jnp.concatenate([jnp.where(m, block, zero) for m in masks], axis=0)

    factor2 = HD ** (-0.5) * LOG2E

    def forward(g, w):
        q = qkv[g, w]
        k = qkv[4 + g, w]
        v_t = qkv[8 + g, w].T
        st = mm(k, stack_heads(q), NT)
        cols = pl.ds(pl.multiple_of(w * WIN, WIN), WIN)
        for h in range(4):
            z = st[:, h * 128:(h + 1) * 128] * factor2 + bias[4 * g + h]
            e = jnp.exp2(z - jnp.max(z, axis=0, keepdims=True))
            p = (e * (1.0 / jnp.sum(e, axis=0, keepdims=True))).astype(BF16)
            soft[g, w, :, h * 128:(h + 1) * 128] = p
            a = mm(v_t[h * HD:(h + 1) * HD], p)
            att_t[pl.ds(pl.multiple_of(g * 128 + h * HD, HD), HD), cols] = a.astype(BF16)

    def fwd_step(it, _):
        forward(it // NWIN, it % NWIN)
        return 0

    lax.fori_loop(0, GROUPS * NWIN, fwd_step, 0)

    def order_rows(m, _):
        cols = pl.ds(pl.multiple_of(m * 256, 256), 256)
        att_p[:, cols] = mm(order, att_t[:, cols]).astype(BF16)
        return 0

    lax.fori_loop(0, 4, order_rows, 0)

    def proj_grad(m, _):
        rows = pl.ds(pl.multiple_of(m * 128, 128), 128)
        y = (mm(att_p[rows, :], dw[...].reshape(TOK, C)) * grad_scale).astype(BF16)
        half = m // 2
        for n in range(2):
            for b in range(4):
                k = n * 64 + b * 16
                pieces[0].s0[half, 2 * (m % 2) + n, b] = y[k:k + 16]
        return 0

    lax.fori_loop(0, 4, proj_grad, 0)
    pieces[0].start()

    factor = HD ** (-0.5)

    def backward(g, w):
        q = qkv[g, w]
        k = qkv[4 + g, w]
        v = qkv[8 + g, w]
        dhm = stack_heads(dh[g, w])
        k_t = k.T
        p_all = soft[g, w]
        ds_t = mm(v, dhm, NT)
        low = []
        dq_t = []
        for h in range(4):
            hs = slice(h * 128, (h + 1) * 128)
            p = p_all[:, hs].astype(F32)
            t = p * ds_t[:, hs]
            dsc = t - p * jnp.sum(t, axis=0, keepdims=True)
            dsum[:, hs] = dsum[:, hs] + dsc
            lo = dsc.astype(BF16)
            low.append(lo)
            dq_t.append(mm(k_t[h * HD:(h + 1) * HD], lo))
        dv = mm(p_all, dhm)
        dk = mm(jnp.concatenate(low, axis=1), stack_heads(q)) * factor
        dq = (jnp.concatenate(dq_t, axis=0) * factor).T
        dproj[w, :, 0:128] = dq.astype(BF16)
        dproj[w, :, 128:256] = dk.astype(BF16)
        dproj[w, :, 256:384] = dv.astype(BF16)

    def store(p):
        total, table_sum = pieces[p].step4()
        if p == 0:
            gp_ref[...] = total
        else:
            for b in range(3):
                gq_ref[:, b * C + (p - 1) * 128:b * C + p * 128] = total[:, b * 128:(b + 1) * 128]
            g4[4 * (p - 1):4 * p] = table_sum

    for g in range(GROUPS):
        dsum[...] = jnp.zeros_like(dsum)

        def bwd_step(w, _):
            backward(g, w)
            pl.when(w == 1)(pieces[g].step1)
            pl.when(w == 3)(pieces[g].step2)
            pl.when(w == 5)(pieces[g].step3)
            return 0

        lax.fori_loop(0, NWIN, bwd_step, 0)
        store(g)

        flipped = sum(mm(reverse, part) for part in split3(dsum[...]))
        heads = []
        for h in range(4):
            u = pltpu.roll(flipped[:, h * 128:(h + 1) * 128], 1, 1, stride=1, stride_axis=0)
            cells = []
            for q in range(4):
                keep = (wrap_r if q // 2 else ~wrap_r) & (carry_r if q % 2 else ~carry_r)
                cells.append(jnp.sum(jnp.where(keep, u, 0.0), axis=0, keepdims=True))
            heads.append(jnp.concatenate(cells, axis=1))

        def weight_grad(m, _):
            rows = pl.ds(pl.multiple_of(m * 128, 128), 128)
            y = (mm(normed_t[rows, :], dproj[...].reshape(TOK, 384)) * grad_scale).astype(BF16)
            half = m // 2
            for n in range(2):
                for b in range(4):
                    k = n * 64 + b * 16
                    pieces[g + 1].s0[half, 2 * (m % 2) + n, b] = y[k:k + 16]
            return 0

        lax.fori_loop(0, 4, weight_grad, 0)
        pieces[g + 1].start(jnp.concatenate(heads, axis=0))

        def norm_grad(m, _):
            lhs = dproj[pl.ds(2 * m, 2)].reshape(256, 384)
            w_cols = jnp.concatenate(
                [wqkv_ref[:, b * C + g * 128:b * C + (g + 1) * 128] for b in range(3)], axis=1
            )
            y = mm(lhs, w_cols, NT).reshape(2, WIN, C)
            if g == 0:
                dnorm[pl.ds(2 * m, 2)] = y
            else:
                dnorm[pl.ds(2 * m, 2)] = dnorm[pl.ds(2 * m, 2)] + y
            return 0

        lax.fori_loop(0, 4, norm_grad, 0)

    last = pieces[GROUPS]

    def finish(w, _):
        n = nx[w]
        sc = dnorm[w] * gain
        m1 = jnp.mean(sc, axis=-1, keepdims=True)
        m2 = jnp.mean(sc * n, axis=-1, keepdims=True)
        branch = istd[w] * (sc - m1 - n * m2)
        ow[w] = (dw[w].astype(F32) + branch).astype(BF16)
        return 0

    finish(0, 0)
    home = remote(ow.at[0], back_ref, halo_send.at[2], halo_recv.at[2], here.slab(-1))
    home.start()
    last.step1()
    lax.fori_loop(1, NWIN, finish, 0)
    last.step2()

    to_slab = one_hot(c_i == w_i + s)
    edge_slab = one_hot(t_c == t_w + s - 16)

    def out_row(r, _):
        rows = pl.ds(pl.multiple_of(r * WW, WW), WW)
        src = jnp.concatenate([ow[w, rows, :] for w in range(NWIN)], axis=0)
        out_ref[r] = mm(to_slab, src).astype(BF16)
        return 0

    lax.fori_loop(0, WH, out_row, 0)
    last.step3()

    home.wait_recv()

    def edge_row(r, _):
        rows = pl.ds(pl.multiple_of(r * WW, WW), WW)
        y = mm(edge_slab, back_ref[rows, :]).astype(BF16)
        out_ref[r, COLS - WW:, :] = out_ref[r, COLS - WW:, :] + y
        return 0

    lax.fori_loop(0, WH, edge_row, 0)

    pick = iota((16, C), 1) == 2 * (here.lon * 4 + here.lat) + iota((16, C), 0)
    w_rows = mm(one_hot(pick), wqkv_ref[...])[0:2]
    gain_rows = jnp.sum(jnp.where(pick, jnp.broadcast_to(gain, (16, C)), 0.0), axis=1, keepdims=True)[0:2]

    store(GROUPS)
    gg_ref[...] = jnp.sum(gq_ref[...] * w_rows, axis=1, keepdims=True) / gain_rows

    parts = split3(g4[...])
    total = mm(hot[...], parts[0], NT) + mm(hot[...], parts[1], NT) + mm(hot[...], parts[2], NT)
    gt_ref[...] = total[0:NREL] * ((TOK * n_dev) // WIN) ** (-0.5)

    for piece in pieces:
        piece.finish()
    for copy in halo + [home]:
        copy.wait_send()


def piece_scratch(width):
    return [
        pltpu.VMEM((2, 4, 4, 16, width), BF16),
        pltpu.VMEM((4, 4, 16, width), BF16),
        pltpu.VMEM((4, 4, 16, width), BF16),
        pltpu.VMEM((3, 4, 16, width), BF16),
        pltpu.VMEM((4, 16, width), BF16),
        pltpu.VMEM((3, 16, width), BF16),
        pltpu.VMEM((NZ, 2, width), F32),
        pltpu.VMEM((NZ - 1, 2, width), F32),
        pltpu.SemaphoreType.DMA((14,)),
        pltpu.SemaphoreType.DMA((14,)),
    ]


def table_scratch():
    counts = (2, 4, 4, NZ)
    return (
        [pltpu.VMEM((n, 4, 512), F32) for n in counts]
        + [pltpu.SemaphoreType.DMA((n,)) for n in counts]
        + [pltpu.SemaphoreType.DMA((n,)) for n in counts]
    )


def fused(n_dev, *args):
    vm = pl.BlockSpec(memory_space=pltpu.VMEM)
    return pl.pallas_call(
        functools.partial(body, n_dev),
        out_shape=(
            jax.ShapeDtypeStruct((WH, COLS, C), BF16),
            jax.ShapeDtypeStruct((2, 3 * C), F32),
            jax.ShapeDtypeStruct((2, C), F32),
            jax.ShapeDtypeStruct((2, 1), F32),
            jax.ShapeDtypeStruct((NREL, H), F32),
        ),
        in_specs=[pl.BlockSpec(memory_space=pltpu.SMEM)] + [vm] * 7,
        out_specs=(vm,) * 5,
        scratch_shapes=[
            pltpu.VMEM((NWIN, WIN, C), BF16),
            pltpu.VMEM((NWIN, WIN, C), BF16),
            pltpu.VMEM((NWIN, WIN, C), F32),
            pltpu.VMEM((NWIN, WIN, 1), F32),
            pltpu.VMEM((NWIN, WIN, C), BF16),
            pltpu.VMEM((C, TOK), BF16),
            pltpu.VMEM((12, NWIN, WIN, 128), BF16),
            pltpu.VMEM((GROUPS, NWIN, WIN, 128), BF16),
            pltpu.VMEM((GROUPS, NWIN, WIN, 512), BF16),
            pltpu.VMEM((C, TOK), BF16),
            pltpu.VMEM((NWIN, WIN, 384), BF16),
            pltpu.VMEM((NWIN, WIN, C), F32),
            pltpu.VMEM((WIN, 512), F32),
            pltpu.VMEM((H, WIN, WIN), F32),
            pltpu.VMEM((512, 512), BF16),
            pltpu.VMEM((H, 512), F32),
            pltpu.VMEM((NWIN, WIN, C), BF16),
            pltpu.VMEM((C, TOK), BF16),
            pltpu.VMEM((WH, WW, C), BF16),
            pltpu.VMEM((WH, WW, C), BF16),
            pltpu.VMEM((WIN, C), BF16),
            pltpu.SemaphoreType.DMA((3,)),
            pltpu.SemaphoreType.DMA((3,)),
        ]
        + [ref for width in PIECES for ref in piece_scratch(width)]
        + [ref for _ in range(GROUPS) for ref in table_scratch()],
        compiler_params=pltpu.CompilerParams(
            vmem_limit_bytes=58 * 1024 * 1024, collective_id=0, has_side_effects=True
        ),
        name="fused",
    )(*args)


def shards(inputs, d_out, w_qkv, w_proj, gain, bias_table, rel_index, shifts):
    n_dev = lax.axis_size("lon") * lax.axis_size("lat")
    d_inputs, gq, gp, gg, gt = fused(
        n_dev, shifts, inputs, d_out, w_qkv, w_proj, gain.reshape(1, C), bias_table, rel_index
    )
    return (d_inputs, gq, gp, gg.reshape(2), gt)


def solution(mesh):
    return jax.shard_map(
        shards,
        mesh=mesh,
        in_specs=(P("lat", "lon", None), P("lat", "lon", None), P(), P(), P(), P(), P(), P("lat")),
        out_specs=(
            P("lat", "lon", None),
            P(("lon", "lat"), None),
            P(("lon", "lat"), None),
            P(("lon", "lat")),
            P(),
        ),
        check_vma=False,
    )
```

profile of v0, /device:TPU:8, one launch (start us, length us, event | category | flops | bytes accessed | tf_op | source)
XLA Modules:
  0.0 135.9 jit_solution(5548948386320515997)
XLA Ops:
  1.3 1.6 %copy.15.table_ref = f32[465,16]{1,0:T(8,128)} copy(f32[465,16]{0,1:T(8,128)} %param.13) | data formatting | bytes 59520 | tf_op args[5]
  2.9 126.6 %fused.1 = (bf16[8,128,512]{2,1,0:T(8,128)(2,1)}, f32[2,1536]{1,0:T(2,128)}, f32[2,512]{1,0:T(2,128)}, f32[2,1]{1,0:T(2,128)}, f32[465,16]{1,0:T(8,128)}) custom-call(s32[1]{0:T(128)S(6)} %copy.20.shift_ref, bf16[8,128,512]{2,1,0:T(8,128)(2,1)} %x_ref.1, bf16[8,128,512]{2,1,0:T(8,128)(2,1)} %d_ref.1, bf16[512,1536]{1,0:T(8,128)(2,1)} %wqkv_ref.1, ...), custom_call_target="tpu_custom_call" | custom-call | tf_op jit(solution)/shard_map/fused/pallas_call | solution.py:559
  129.4 0.0 copy-start
  129.4 0.0 copy-start.1
  129.4 1.3 reduce
  130.7 1.7 %copy.16 = f32[465,16]{0,1:T(8,128)} copy(f32[465,16]{1,0:T(8,128)} %get-tuple-element.24) | data formatting | bytes 59520
  132.4 2.3 %copy.21 = bf16[8,128,512]{2,1,0:T(8,128)(2,1)} copy(bf16[8,128,512]{2,1,0:T(8,128)(2,1)} %get-tuple-element.30) | data formatting | bytes 2097152
  134.7 0.0 copy-done
  134.7 0.6 copy.22
  135.3 0.0 copy-done.1
  135.3 0.6 copy.23
Async XLA Ops:
  129.4 5.2 %copy-start = (f32[2,1536]{1,0:T(2,128)S(1)}, f32[2,1536]{1,0:T(2,128)}, u32[]{:S(2)}) copy-start(f32[2,1536]{1,0:T(2,128)} %get-tuple-element.31) | copy-start | bytes 36868
  129.4 5.8 %copy-start.1 = (f32[2,512]{1,0:T(2,128)S(1)}, f32[2,512]{1,0:T(2,128)}, u32[]{:S(2)}) copy-start(f32[2,512]{1,0:T(2,128)} %get-tuple-element.32) | copy-start | bytes 12292
where the time goes:
time: 136 us
  Pallas kernels  127 us (93%)
  local copies, waits for them, and re-layouts  6.71 us (5%)
    pallas_call x1, Pallas kernels, fused(): pl.pallas_call(functools.partial(body, n_dev), out_shape=(jax.ShapeDtypeS...  127 us
    unnamed x9, local copies, waits for them, and re-layouts  6.71 us

commit v1 on v0

--- a/solution.py
+++ b/solution.py
@@ -61,7 +61,7 @@
 
 NX, NY, NZ = 4, 4, 8
 PIECES = (C, 384, 384, 384, 384)
-X_FIRST = (True, False, True, False, True)
+TABLE_GROUPS = {3: (0, 1, 2), 4: (3,)}
 
 
 class Place:
@@ -73,6 +73,8 @@
         self.x = (lon // 32) * 2 + lat // 2
         self.z = lax.rem(lon // 4, 8)
         self.y = lax.rem(lon, 4)
+        self.a = self.x + self.core * (self.y - self.x)
+        self.b = self.y + self.core * (self.x - self.y)
 
     def at(self, x=None, y=None, z=None, core=None):
         x = self.x if x is None else x
@@ -87,10 +89,11 @@
     def along(self, axis, step):
         if axis == "core":
             return self.partner()
-        if axis == "x":
-            return self.at(x=lax.rem(self.x + step, NX))
-        if axis == "y":
-            return self.at(y=lax.rem(self.y + step, NY))
+        if axis in "ab":
+            to_y = self.core if axis == "a" else 1 - self.core
+            return self.at(
+                x=lax.rem(self.x + (1 - to_y) * step, NX), y=lax.rem(self.y + to_y * step, NY)
+            )
         return self.at(z=lax.rem(self.z + step, NZ))
 
     def slab(self, step):
@@ -105,12 +108,13 @@
 
 
 class Reduction:
-    def __init__(self, here, refs, x_first, table):
+    axes = ("core", "a", "b", "z")
+    counts = (2, 4, 4, NZ)
+
+    def __init__(self, here, refs, table):
         self.here = here
         (self.s0, self.r0, self.s1, self.r1, self.s2, self.r2, self.s3, self.r3,
          self.send, self.recv) = refs
-        self.axes = ("core", "x", "y", "z") if x_first else ("core", "y", "x", "z")
-        self.counts = (2, 4, 4, NZ)
         self.table = table
 
     def copies(self, stage):
@@ -122,8 +126,7 @@
             if stage == 0:
                 src, dst = self.s0.at[target], self.r0
             elif stage == 1:
-                src = self.s1.at[target] if axis == "x" else self.s1.at[:, target]
-                dst = self.r1.at[step - 1]
+                src, dst = self.s1.at[target], self.r1.at[step - 1]
             elif stage == 2:
                 src, dst = self.s2.at[target], self.r2.at[step - 1]
             else:
@@ -152,7 +155,7 @@
         for copy in self.copies(stage):
             copy.start()
         if self.table is not None:
-            self.table[0][stage][getattr(self.here, self.axes[stage])] = table_value
+            self.table[0][stage][getattr(self.here, self.axes[stage])] = table_value.astype(BF16)
             for copy in self.table_copies(stage, False):
                 copy.start()
 
@@ -164,9 +167,9 @@
         if self.table is None:
             return None
         slots = self.table[0][stage]
-        total = slots[0]
+        total = slots[0].astype(F32)
         for n in range(1, self.counts[stage]):
-            total = total + slots[n]
+            total = total + slots[n].astype(F32)
         return total
 
     def start(self, table_value=None):
@@ -182,8 +185,7 @@
     def step2(self):
         table_value = self.arrived(1)
         for n in range(4):
-            own = self.s1[self.here.x, n] if self.axes[1] == "x" else self.s1[n, self.here.y]
-            total = own.astype(F32)
+            total = self.s1[self.here.a, n].astype(F32)
             for r in range(3):
                 total = total + self.r1[r, n].astype(F32)
             self.s2[n] = total.astype(BF16)
@@ -191,7 +193,7 @@
 
     def step3(self):
         table_value = self.arrived(2)
-        total = self.s2[getattr(self.here, self.axes[2])].astype(F32)
+        total = self.s2[self.here.b].astype(F32)
         for r in range(3):
             total = total + self.r2[r].astype(F32)
         for z in range(NZ):
@@ -220,30 +222,20 @@
 ):
     here = Place()
     peers = [here.partner(), here.slab(1), here.slab(-1)]
-    peers += [here.along("x", n) for n in range(1, NX)]
-    peers += [here.along("y", n) for n in range(1, NY)]
+    peers += [here.along("a", n) for n in range(1, NX)]
+    peers += [here.along("b", n) for n in range(1, NY)]
     peers += [here.along("z", n) for n in range(1, NZ)]
     barrier = pltpu.get_barrier_semaphore()
     for peer in peers:
         pl.semaphore_signal(barrier, inc=1, device_id=peer, device_id_type=pl.DeviceIdType.MESH)
-    pl.semaphore_wait(barrier, len(peers))
-
-    edge = pl.ds(COLS - WW, WW)
-    halo = [
-        remote(src.at[:, edge, :], dst, halo_send.at[n], halo_recv.at[n], here.slab(1))
-        for n, (src, dst) in enumerate(((x_ref, tx_ref), (d_ref, td_ref)))
-    ]
-    for copy in halo:
-        copy.start()
-
     pieces = []
     for p in range(len(PIECES)):
         refs = rest[p * 10:(p + 1) * 10]
         table = None
-        if p:
-            base = len(PIECES) * 10 + (p - 1) * 12
+        if p in TABLE_GROUPS:
+            base = len(PIECES) * 10 + 12 * list(TABLE_GROUPS).index(p)
             table = (rest[base:base + 4], rest[base + 4:base + 8], rest[base + 8:base + 12])
-        pieces.append(Reduction(here, refs, X_FIRST[p], table))
+        pieces.append(Reduction(here, refs, table))
 
     s = shift_ref[0]
     w_i = iota((128, 128), 0)
@@ -265,6 +257,16 @@
 
     lax.fori_loop(0, WH, shift_row, 0)
 
+    pl.semaphore_wait(barrier, len(peers))
+
+    edge = pl.ds(COLS - WW, WW)
+    halo = [
+        remote(src.at[:, edge, :], dst, halo_send.at[n], halo_recv.at[n], here.slab(1))
+        for n, (src, dst) in enumerate(((x_ref, tx_ref), (d_ref, td_ref)))
+    ]
+    for copy in halo:
+        copy.start()
+
     rel_t = rel_ref[...].astype(F32).T
     code_rows = []
     for wrap in (0, 1):
@@ -274,8 +276,7 @@
             code_rows.append(pltpu.roll(jnp.broadcast_to(row, (8, 128)), (128 - j) % 128, 1)[0:1])
     code = jnp.concatenate(code_rows, axis=1).astype(jnp.int32)
     hot[...] = one_hot(iota((512, 512), 0) == code)
-    tab = jnp.concatenate([table_ref[...], jnp.zeros((512 - NREL, H), F32)], axis=0).T
-    tab = tab * LOG2E
+    tab = jnp.concatenate([table_ref[...] * LOG2E, jnp.zeros((H, 512 - NREL), F32)], axis=1)
     parts = split3(tab)
     t4 = mm(parts[0], hot[...]) + mm(parts[1], hot[...]) + mm(parts[2], hot[...])
     g4[...] = t4
@@ -301,10 +302,12 @@
         normed[w] = (n * gain).astype(BF16)
         return 0
 
-    lax.fori_loop(1, NWIN, norm_win, 0)
+    lax.fori_loop(2, NWIN, norm_win, 0)
 
     row_p = iota((C, C), 0)
-    p_core, p_x, p_y = row_p // 256, (row_p // 64) % 4, (row_p // 16) % 4
+    p_core, p_a, p_b = row_p // 256, (row_p // 64) % 4, (row_p // 16) % 4
+    p_x = p_a + p_core * (p_b - p_a)
+    p_y = p_b + p_core * (p_a - p_b)
     p_z, p_t = (row_p // 2) % 8, row_p % 2
     source = (p_x // 2) * 256 + p_z * 32 + p_y * 8 + (p_x % 2) * 4 + p_core * 2 + p_t
     order = one_hot(iota((C, C), 1) == source)
@@ -324,20 +327,6 @@
         return 0
 
     lax.fori_loop(1, 4, project, 0)
-    for copy in halo:
-        copy.wait_recv()
-
-    def tail_row(r, _):
-        rows = pl.ds(pl.multiple_of(r * WW, WW), WW)
-        for src, dst in ((tx_ref, xw), (td_ref, dw)):
-            y = mm(tail_win, src[r]).astype(BF16)
-            dst[0, rows, :] = dst[0, rows, :] + y
-        return 0
-
-    lax.fori_loop(0, WH, tail_row, 0)
-    norm_win(0, 0)
-    project(0, 0)
-
     masks = head_masks(128)
 
     def stack_heads(block):
@@ -361,10 +350,30 @@
             att_t[pl.ds(pl.multiple_of(g * 128 + h * HD, HD), HD), cols] = a.astype(BF16)
 
     def fwd_step(it, _):
-        forward(it // NWIN, it % NWIN)
-        return 0
-
-    lax.fori_loop(0, GROUPS * NWIN, fwd_step, 0)
+        forward(it // (NWIN - 2), 2 + it % (NWIN - 2))
+        return 0
+
+    lax.fori_loop(0, GROUPS * (NWIN - 2), fwd_step, 0)
+
+    for copy in halo:
+        copy.wait_recv()
+
+    def tail_row(r, _):
+        rows = pl.ds(pl.multiple_of(r * WW, WW), WW)
+        for src, dst in ((tx_ref, xw), (td_ref, dw)):
+            y = mm(tail_win, src[r]).astype(BF16)
+            dst[0, rows, :] = dst[0, rows, :] + y
+        return 0
+
+    lax.fori_loop(0, WH, tail_row, 0)
+    lax.fori_loop(0, 2, norm_win, 0)
+    project(0, 0)
+
+    def fwd_late(it, _):
+        forward(it // 2, it % 2)
+        return 0
+
+    lax.fori_loop(0, GROUPS * 2, fwd_late, 0)
 
     def order_rows(m, _):
         cols = pl.ds(pl.multiple_of(m * 256, 256), 256)
@@ -410,9 +419,9 @@
         dv = mm(p_all, dhm)
         dk = mm(jnp.concatenate(low, axis=1), stack_heads(q)) * factor
         dq = (jnp.concatenate(dq_t, axis=0) * factor).T
-        dproj[w, :, 0:128] = dq.astype(BF16)
-        dproj[w, :, 128:256] = dk.astype(BF16)
-        dproj[w, :, 256:384] = dv.astype(BF16)
+        dproj[0, g, w] = dq.astype(BF16)
+        dproj[1, g, w] = dk.astype(BF16)
+        dproj[2, g, w] = dv.astype(BF16)
 
     def store(p):
         total, table_sum = pieces[p].step4()
@@ -421,34 +430,42 @@
         else:
             for b in range(3):
                 gq_ref[:, b * C + (p - 1) * 128:b * C + p * 128] = total[:, b * 128:(b + 1) * 128]
-            g4[4 * (p - 1):4 * p] = table_sum
-
+        if p in TABLE_GROUPS:
+            for n, group in enumerate(TABLE_GROUPS[p]):
+                for h in range(4):
+                    for q in range(4):
+                        r = 16 * n + 4 * h + q
+                        g4[4 * group + h:4 * group + h + 1, q * 128:(q + 1) * 128] = table_sum[r:r + 1]
+
+    bias_sums = {}
     for g in range(GROUPS):
         dsum[...] = jnp.zeros_like(dsum)
 
         def bwd_step(w, _):
             backward(g, w)
-            pl.when(w == 1)(pieces[g].step1)
-            pl.when(w == 3)(pieces[g].step2)
-            pl.when(w == 5)(pieces[g].step3)
+            if g:
+                pl.when(w == 1)(pieces[g - 1].step3)
+                pl.when(w == 5)(functools.partial(store, g - 1))
+            pl.when(w == 2)(pieces[g].step1)
+            pl.when(w == 7)(pieces[g].step2)
             return 0
 
         lax.fori_loop(0, NWIN, bwd_step, 0)
-        store(g)
 
         flipped = sum(mm(reverse, part) for part in split3(dsum[...]))
-        heads = []
+        heads = bias_sums.setdefault(min(p for p in TABLE_GROUPS if g in TABLE_GROUPS[p]), [])
         for h in range(4):
             u = pltpu.roll(flipped[:, h * 128:(h + 1) * 128], 1, 1, stride=1, stride_axis=0)
-            cells = []
             for q in range(4):
                 keep = (wrap_r if q // 2 else ~wrap_r) & (carry_r if q % 2 else ~carry_r)
-                cells.append(jnp.sum(jnp.where(keep, u, 0.0), axis=0, keepdims=True))
-            heads.append(jnp.concatenate(cells, axis=1))
+                heads.append(jnp.sum(jnp.where(keep, u, 0.0), axis=0, keepdims=True))
 
         def weight_grad(m, _):
             rows = pl.ds(pl.multiple_of(m * 128, 128), 128)
-            y = (mm(normed_t[rows, :], dproj[...].reshape(TOK, 384)) * grad_scale).astype(BF16)
+            y = jnp.concatenate(
+                [mm(normed_t[rows, :], dproj[b, g].reshape(TOK, 128)) for b in range(3)], axis=1
+            )
+            y = (y * grad_scale).astype(BF16)
             half = m // 2
             for n in range(2):
                 for b in range(4):
@@ -457,21 +474,17 @@
             return 0
 
         lax.fori_loop(0, 4, weight_grad, 0)
-        pieces[g + 1].start(jnp.concatenate(heads, axis=0))
-
-        def norm_grad(m, _):
-            lhs = dproj[pl.ds(2 * m, 2)].reshape(256, 384)
-            w_cols = jnp.concatenate(
-                [wqkv_ref[:, b * C + g * 128:b * C + (g + 1) * 128] for b in range(3)], axis=1
-            )
-            y = mm(lhs, w_cols, NT).reshape(2, WIN, C)
-            if g == 0:
-                dnorm[pl.ds(2 * m, 2)] = y
-            else:
-                dnorm[pl.ds(2 * m, 2)] = dnorm[pl.ds(2 * m, 2)] + y
-            return 0
-
-        lax.fori_loop(0, 4, norm_grad, 0)
+        pieces[g + 1].start(
+            jnp.concatenate(bias_sums[g + 1], axis=0) if g + 1 in TABLE_GROUPS else None
+        )
+
+    def norm_grad(m, _):
+        lhs = jnp.concatenate(
+            [dproj[b, g, pl.ds(2 * m, 2)].reshape(256, 128) for b in range(3) for g in range(GROUPS)],
+            axis=1,
+        )
+        dnorm[pl.ds(2 * m, 2)] = mm(lhs, wqkv_ref[...], NT).reshape(2, WIN, C)
+        return 0
 
     last = pieces[GROUPS]
 
@@ -484,12 +497,16 @@
         ow[w] = (dw[w].astype(F32) + branch).astype(BF16)
         return 0
 
+    norm_grad(0, 0)
     finish(0, 0)
     home = remote(ow.at[0], back_ref, halo_send.at[2], halo_recv.at[2], here.slab(-1))
     home.start()
+    pieces[GROUPS - 1].step3()
     last.step1()
+    lax.fori_loop(1, 4, norm_grad, 0)
+    store(GROUPS - 1)
+    last.step2()
     lax.fori_loop(1, NWIN, finish, 0)
-    last.step2()
 
     to_slab = one_hot(c_i == w_i + s)
     edge_slab = one_hot(t_c == t_w + s - 16)
@@ -500,8 +517,8 @@
         out_ref[r] = mm(to_slab, src).astype(BF16)
         return 0
 
+    last.step3()
     lax.fori_loop(0, WH, out_row, 0)
-    last.step3()
 
     home.wait_recv()
 
@@ -518,11 +535,12 @@
     gain_rows = jnp.sum(jnp.where(pick, jnp.broadcast_to(gain, (16, C)), 0.0), axis=1, keepdims=True)[0:2]
 
     store(GROUPS)
-    gg_ref[...] = jnp.sum(gq_ref[...] * w_rows, axis=1, keepdims=True) / gain_rows
+    gg = jnp.sum(gq_ref[...] * w_rows, axis=1, keepdims=True) / gain_rows
+    gg_ref[...] = jnp.where(iota((1, 2), 1) == 0, gg[0:1], gg[1:2])
 
     parts = split3(g4[...])
-    total = mm(hot[...], parts[0], NT) + mm(hot[...], parts[1], NT) + mm(hot[...], parts[2], NT)
-    gt_ref[...] = total[0:NREL] * ((TOK * n_dev) // WIN) ** (-0.5)
+    total = mm(parts[0], hot[...], NT) + mm(parts[1], hot[...], NT) + mm(parts[2], hot[...], NT)
+    gt_ref[...] = total[:, 0:NREL] * ((TOK * n_dev) // WIN) ** (-0.5)
 
     for piece in pieces:
         piece.finish()
@@ -545,10 +563,10 @@
     ]
 
 
-def table_scratch():
-    counts = (2, 4, 4, NZ)
+def table_scratch(groups):
+    counts = Reduction.counts
     return (
-        [pltpu.VMEM((n, 4, 512), F32) for n in counts]
+        [pltpu.VMEM((n, 16 * groups, 128), BF16) for n in counts]
         + [pltpu.SemaphoreType.DMA((n,)) for n in counts]
         + [pltpu.SemaphoreType.DMA((n,)) for n in counts]
     )
@@ -562,8 +580,8 @@
             jax.ShapeDtypeStruct((WH, COLS, C), BF16),
             jax.ShapeDtypeStruct((2, 3 * C), F32),
             jax.ShapeDtypeStruct((2, C), F32),
-            jax.ShapeDtypeStruct((2, 1), F32),
-            jax.ShapeDtypeStruct((NREL, H), F32),
+            jax.ShapeDtypeStruct((1, 2), F32),
+            jax.ShapeDtypeStruct((H, NREL), F32),
         ),
         in_specs=[pl.BlockSpec(memory_space=pltpu.SMEM)] + [vm] * 7,
         out_specs=(vm,) * 5,
@@ -578,7 +596,7 @@
             pltpu.VMEM((GROUPS, NWIN, WIN, 128), BF16),
             pltpu.VMEM((GROUPS, NWIN, WIN, 512), BF16),
             pltpu.VMEM((C, TOK), BF16),
-            pltpu.VMEM((NWIN, WIN, 384), BF16),
+            pltpu.VMEM((3, GROUPS, NWIN, WIN, 128), BF16),
             pltpu.VMEM((NWIN, WIN, C), F32),
             pltpu.VMEM((WIN, 512), F32),
             pltpu.VMEM((H, WIN, WIN), F32),
@@ -593,7 +611,7 @@
             pltpu.SemaphoreType.DMA((3,)),
         ]
         + [ref for width in PIECES for ref in piece_scratch(width)]
-        + [ref for _ in range(GROUPS) for ref in table_scratch()],
+        + [ref for groups in TABLE_GROUPS.values() for ref in table_scratch(len(groups))],
         compiler_params=pltpu.CompilerParams(
             vmem_limit_bytes=58 * 1024 * 1024, collective_id=0, has_side_effects=True
         ),
@@ -604,9 +622,9 @@
 def shards(inputs, d_out, w_qkv, w_proj, gain, bias_table, rel_index, shifts):
     n_dev = lax.axis_size("lon") * lax.axis_size("lat")
     d_inputs, gq, gp, gg, gt = fused(
-        n_dev, shifts, inputs, d_out, w_qkv, w_proj, gain.reshape(1, C), bias_table, rel_index
+        n_dev, shifts, inputs, d_out, w_qkv, w_proj, gain.reshape(1, C), bias_table.T, rel_index
     )
-    return (d_inputs, gq, gp, gg.reshape(2), gt)
+    return (d_inputs, gq, gp, gg.reshape(2), gt.T)
 
 
 def solution(mesh):

time: 136 us -> 96.7 us (0.71)
  Pallas kernels: 127 us -> 90.5 us
  local copies, waits for them, and re-layouts: 6.71 us -> 4.6 us
    pallas_call x1, Pallas kernels: 127 us -> 90.5 us  [fused(): pl.pallas_call(functools.partial(body, n_dev), out_shape=(jax.ShapeDtypeS...]
    unnamed x9 -> x13, local copies, waits for them, and re-layouts: 6.71 us -> 4.6 us
where the time goes in v1:
time: 96.7 us; the launch traced here: 96.4 us
  Pallas kernels  90.5 us (94%)
  local copies, waits for them, and re-layouts  4.6 us (5%)
  between operations  1.32 us (1%)
    pallas_call x1, Pallas kernels, fused(): pl.pallas_call(functools.partial(body, n_dev), out_shape=(jax.ShapeDtypeS...  90.5 us
    unnamed x13, local copies, waits for them, and re-layouts  4.6 us

profile of v1, /device:TPU:8, one launch (start us, length us, event | category | flops | bytes accessed | tf_op | source)
XLA Modules:
  0.0 96.4 jit_solution(17650020704682270794)
XLA Ops:
  1.3 90.5 %fused.1 = (bf16[8,128,512]{2,1,0:T(8,128)(2,1)}, f32[2,1536]{1,0:T(2,128)}, f32[2,512]{1,0:T(2,128)}, f32[1,2]{1,0:T(1,128)}, f32[16,465]{1,0:T(8,128)}) custom-call(s32[1]{0:T(128)S(6)} %copy.18.shift_ref, bf16[8,128,512]{2,1,0:T(8,128)(2,1)} %x_ref.1, bf16[8,128,512]{2,1,0:T(8,128)(2,1)} %d_ref.1, bf16[512,1536]{1,0:T(8,128)(2,1)} %wqkv_ref.1, ...), custom_call_target="tpu_custom_call" | custom-call | tf_op jit(solution)/shard_map/fused/pallas_call | solution.py:577
  91.8 0.0 copy-start.1
  91.8 0.0 copy-start.2
  91.8 0.0 copy-start.3
  91.8 0.0 copy-start
  91.8 2.3 %copy.19 = bf16[8,128,512]{2,1,0:T(8,128)(2,1)} copy(bf16[8,128,512]{2,1,0:T(8,128)(2,1)} %get-tuple-element.20) | data formatting | bytes 2097152
  94.1 0.0 copy-done.1
  94.1 0.6 copy.20
  94.7 0.0 copy-done.2
  94.7 0.6 copy.21
  95.3 0.0 copy-done.3
  95.3 0.5 copy.22
  95.8 0.0 copy-done
  95.8 0.6 copy.23
Async XLA Ops:
  91.8 2.3 %copy-start.1 = (f32[2,1536]{1,0:T(2,128)S(1)}, f32[2,1536]{1,0:T(2,128)}, u32[]{:S(2)}) copy-start(f32[2,1536]{1,0:T(2,128)} %get-tuple-element.21) | copy-start | bytes 36868
  91.8 2.9 %copy-start.2 = (f32[2,512]{1,0:T(2,128)S(1)}, f32[2,512]{1,0:T(2,128)}, u32[]{:S(2)}) copy-start(f32[2,512]{1,0:T(2,128)} %get-tuple-element.22) | copy-start | bytes 12292
  91.8 3.5 %copy-start.3 = (f32[1,2]{1,0:T(1,128)S(1)}, f32[1,2]{1,0:T(1,128)}, u32[]{:S(2)}) copy-start(f32[1,2]{1,0:T(1,128)} %get-tuple-element.13) | copy-start | bytes 28
  91.8 4.0 %copy-start = (f32[16,465]{1,0:T(8,128)S(1)}, f32[16,465]{1,0:T(8,128)}, u32[]{:S(2)}) copy-start(f32[16,465]{1,0:T(8,128)} %get-tuple-element.14) | copy-start | bytes 89284

commit v2 on v1

--- a/solution.py
+++ b/solution.py
@@ -350,10 +350,11 @@
             att_t[pl.ds(pl.multiple_of(g * 128 + h * HD, HD), HD), cols] = a.astype(BF16)
 
     def fwd_step(it, _):
-        forward(it // (NWIN - 2), 2 + it % (NWIN - 2))
-        return 0
-
-    lax.fori_loop(0, GROUPS * (NWIN - 2), fwd_step, 0)
+        forward(it // 3, 2 + 2 * (it % 3))
+        forward(it // 3, 3 + 2 * (it % 3))
+        return 0
+
+    lax.fori_loop(0, GROUPS * 3, fwd_step, 0)
 
     for copy in halo:
         copy.wait_recv()
@@ -369,11 +370,12 @@
     lax.fori_loop(0, 2, norm_win, 0)
     project(0, 0)
 
-    def fwd_late(it, _):
-        forward(it // 2, it % 2)
-        return 0
-
-    lax.fori_loop(0, GROUPS * 2, fwd_late, 0)
+    def fwd_late(g, _):
+        forward(g, 0)
+        forward(g, 1)
+        return 0
+
+    lax.fori_loop(0, GROUPS, fwd_late, 0)
 
     def order_rows(m, _):
         cols = pl.ds(pl.multiple_of(m * 256, 256), 256)
@@ -382,17 +384,12 @@
 
     lax.fori_loop(0, 4, order_rows, 0)
 
-    def proj_grad(m, _):
-        rows = pl.ds(pl.multiple_of(m * 128, 128), 128)
-        y = (mm(att_p[rows, :], dw[...].reshape(TOK, C)) * grad_scale).astype(BF16)
-        half = m // 2
-        for n in range(2):
-            for b in range(4):
-                k = n * 64 + b * 16
-                pieces[0].s0[half, 2 * (m % 2) + n, b] = y[k:k + 16]
-        return 0
-
-    lax.fori_loop(0, 4, proj_grad, 0)
+    def to_send(piece, y):
+        y = (y * grad_scale).astype(BF16)
+        for n in range(32):
+            piece.s0[n // 16, (n // 4) % 4, n % 4] = y[n * 16:(n + 1) * 16]
+
+    to_send(pieces[0], mm(att_p[...], dw[...].reshape(TOK, C)))
     pieces[0].start()
 
     factor = HD ** (-0.5)
@@ -441,16 +438,18 @@
     for g in range(GROUPS):
         dsum[...] = jnp.zeros_like(dsum)
 
-        def bwd_step(w, _):
-            backward(g, w)
-            if g:
-                pl.when(w == 1)(pieces[g - 1].step3)
-                pl.when(w == 5)(functools.partial(store, g - 1))
-            pl.when(w == 2)(pieces[g].step1)
-            pl.when(w == 7)(pieces[g].step2)
+        def bwd_step(i, _):
+            backward(g, 2 * i)
+            backward(g, 2 * i + 1)
+            if g >= 1:
+                pl.when(i == 0)(pieces[g - 1].step2)
+            if g >= 2:
+                pl.when(i == 0)(pieces[g - 2].step3)
+                pl.when(i == 3)(functools.partial(store, g - 2))
+            pl.when(i == 1)(pieces[g].step1)
             return 0
 
-        lax.fori_loop(0, NWIN, bwd_step, 0)
+        lax.fori_loop(0, NWIN // 2, bwd_step, 0)
 
         flipped = sum(mm(reverse, part) for part in split3(dsum[...]))
         heads = bias_sums.setdefault(min(p for p in TABLE_GROUPS if g in TABLE_GROUPS[p]), [])
@@ -460,20 +459,8 @@
                 keep = (wrap_r if q // 2 else ~wrap_r) & (carry_r if q % 2 else ~carry_r)
                 heads.append(jnp.sum(jnp.where(keep, u, 0.0), axis=0, keepdims=True))
 
-        def weight_grad(m, _):
-            rows = pl.ds(pl.multiple_of(m * 128, 128), 128)
-            y = jnp.concatenate(
-                [mm(normed_t[rows, :], dproj[b, g].reshape(TOK, 128)) for b in range(3)], axis=1
-            )
-            y = (y * grad_scale).astype(BF16)
-            half = m // 2
-            for n in range(2):
-                for b in range(4):
-                    k = n * 64 + b * 16
-                    pieces[g + 1].s0[half, 2 * (m % 2) + n, b] = y[k:k + 16]
-            return 0
-
-        lax.fori_loop(0, 4, weight_grad, 0)
+        grads = jnp.concatenate([dproj[b, g].reshape(TOK, 128) for b in range(3)], axis=1)
+        to_send(pieces[g + 1], mm(normed_t[...], grads))
         pieces[g + 1].start(
             jnp.concatenate(bias_sums[g + 1], axis=0) if g + 1 in TABLE_GROUPS else None
         )
@@ -501,10 +488,14 @@
     finish(0, 0)
     home = remote(ow.at[0], back_ref, halo_send.at[2], halo_recv.at[2], here.slab(-1))
     home.start()
+    pieces[GROUPS - 2].step3()
+    pieces[GROUPS - 1].step2()
+    last.step1()
+    norm_grad(1, 0)
+    norm_grad(2, 0)
     pieces[GROUPS - 1].step3()
-    last.step1()
-    lax.fori_loop(1, 4, norm_grad, 0)
-    store(GROUPS - 1)
+    norm_grad(3, 0)
+    store(GROUPS - 2)
     last.step2()
     lax.fori_loop(1, NWIN, finish, 0)
 
@@ -520,6 +511,7 @@
     last.step3()
     lax.fori_loop(0, WH, out_row, 0)
 
+    store(GROUPS - 1)
     home.wait_recv()
 
     def edge_row(r, _):
@@ -619,11 +611,45 @@
     )(*args)
 
 
+def handover_body(n, *refs):
+    src, dst, hold = refs[:n], refs[n:2 * n], refs[2 * n:3 * n]
+    sem_in, sem_out = refs[3 * n:]
+
+    def route(a, m, b):
+        rows = [(a[0].at[r], m[0].at[r], b[0].at[r]) for r in range(WH)]
+        return rows + [(a[i], m[i], b[i]) for i in range(1, n)]
+
+    hops = route(src, hold, dst)
+    into = [pltpu.make_async_copy(a, m, sem_in.at[i]) for i, (a, m, _) in enumerate(hops)]
+    out = [pltpu.make_async_copy(m, b, sem_out.at[i]) for i, (_, m, b) in enumerate(hops)]
+    for copy in into:
+        copy.start()
+    for copy, then in zip(into, out):
+        copy.wait()
+        then.start()
+    for copy in out:
+        copy.wait()
+
+
+def handover(*arrays):
+    hbm = pl.BlockSpec(memory_space=pl.ANY)
+    n = len(arrays)
+    return pl.pallas_call(
+        functools.partial(handover_body, n),
+        out_shape=tuple(jax.ShapeDtypeStruct(a.shape, a.dtype) for a in arrays),
+        in_specs=[hbm] * n,
+        out_specs=(hbm,) * n,
+        scratch_shapes=[pltpu.VMEM(a.shape, a.dtype) for a in arrays]
+        + [pltpu.SemaphoreType.DMA((WH + n,)), pltpu.SemaphoreType.DMA((WH + n,))],
+        name="handover",
+    )(*arrays)
+
+
 def shards(inputs, d_out, w_qkv, w_proj, gain, bias_table, rel_index, shifts):
     n_dev = lax.axis_size("lon") * lax.axis_size("lat")
-    d_inputs, gq, gp, gg, gt = fused(
+    d_inputs, gq, gp, gg, gt = handover(*fused(
         n_dev, shifts, inputs, d_out, w_qkv, w_proj, gain.reshape(1, C), bias_table.T, rel_index
-    )
+    ))
     return (d_inputs, gq, gp, gg.reshape(2), gt.T)
 
 

time: 96.7 us -> 78.1 us (0.81)
  Pallas kernels: 90.5 us -> 76.7 us
  local copies, waits for them, and re-layouts: 4.6 us -> 0 us
    pallas_call x1, Pallas kernels: 90.5 us -> 74.5 us  [fused(): pl.pallas_call(functools.partial(body, n_dev), out_shape=(jax.ShapeDtypeS...]
    unnamed x13 -> x0, local copies, waits for them, and re-layouts: 4.6 us -> none
    pallas_call x0 -> x1, Pallas kernels: none -> 2.19 us  [handover(): pl.pallas_call(functools.partial(handover_body, n), out_shape=tuple((jax....]
where the time goes in v2:
time: 78.1 us; the launch traced here: 78 us
  Pallas kernels  76.7 us (98%)
  between operations  1.29 us (2%)
    pallas_call x1, Pallas kernels, fused(): pl.pallas_call(functools.partial(body, n_dev), out_shape=(jax.ShapeDtypeS...  74.5 us
    pallas_call x1, Pallas kernels, handover(): pl.pallas_call(functools.partial(handover_body, n), out_shape=tuple((jax....  2.19 us

profile of v2, /device:TPU:8, one launch (start us, length us, event | category | flops | bytes accessed | tf_op | source)
XLA Modules:
  0.0 78.0 jit_solution(7279323184236232805)
XLA Ops:
  1.3 74.5 %fused.1 = (bf16[8,128,512]{2,1,0:T(8,128)(2,1)}, f32[2,1536]{1,0:T(2,128)}, f32[2,512]{1,0:T(2,128)}, f32[1,2]{1,0:T(1,128)}, f32[16,465]{1,0:T(8,128)}) custom-call(s32[1]{0:T(128)S(6)} %copy.13.shift_ref, bf16[8,128,512]{2,1,0:T(8,128)(2,1)} %x_ref.1, bf16[8,128,512]{2,1,0:T(8,128)(2,1)} %d_ref.1, bf16[512,1536]{1,0:T(8,128)(2,1)} %wqkv_ref.1, ...), custom_call_target="tpu_custom_call" | custom-call | tf_op jit(solution)/shard_map/fused/pallas_call | solution.py:569
  75.8 2.2 %handover.1 = (bf16[8,128,512]{2,1,0:T(8,128)(2,1)}, f32[2,1536]{1,0:T(2,128)}, f32[2,512]{1,0:T(2,128)}, f32[1,2]{1,0:T(1,128)}, f32[16,465]{1,0:T(8,128)}) custom-call(bf16[8,128,512]{2,1,0:T(8,128)(2,1)} %get-tuple-element.15.refs_0_, f32[2,1536]{1,0:T(2,128)} %get-tuple-element.16.refs_1_, f32[2,512]{1,0:T(2,128)} %get-tuple-element.17.refs_2_, ...), custom_call_target="tpu_custom_call" | custom-call | tf_op jit(solution)/shard_map/handover/pallas_call | solution.py:637

commit v3 on v2

--- a/solution.py
+++ b/solution.py
@@ -333,28 +333,35 @@
         zero = jnp.zeros_like(block)
         return jnp.concatenate([jnp.where(m, block, zero) for m in masks], axis=0)
 
+    def head_rows(block):
+        cols = []
+        for h in range(4):
+            rows = [jnp.zeros((HD, block.shape[1]), block.dtype)] * 4
+            rows[h] = block[h * HD:(h + 1) * HD]
+            cols.append(jnp.concatenate(rows, axis=0))
+        return jnp.concatenate(cols, axis=1)
+
     factor2 = HD ** (-0.5) * LOG2E
 
-    def forward(g, w):
-        q = qkv[g, w]
-        k = qkv[4 + g, w]
-        v_t = qkv[8 + g, w].T
-        st = mm(k, stack_heads(q), NT)
-        cols = pl.ds(pl.multiple_of(w * WIN, WIN), WIN)
+    def forward(blocks):
+        scores = [mm(stack_heads(qkv[4 + g, w]), qkv[g, w], NT) for g, w in blocks]
+        probs = [[] for _ in blocks]
         for h in range(4):
-            z = st[:, h * 128:(h + 1) * 128] * factor2 + bias[4 * g + h]
-            e = jnp.exp2(z - jnp.max(z, axis=0, keepdims=True))
-            p = (e * (1.0 / jnp.sum(e, axis=0, keepdims=True))).astype(BF16)
-            soft[g, w, :, h * 128:(h + 1) * 128] = p
-            a = mm(v_t[h * HD:(h + 1) * HD], p)
-            att_t[pl.ds(pl.multiple_of(g * 128 + h * HD, HD), HD), cols] = a.astype(BF16)
-
-    def fwd_step(it, _):
-        forward(it // 3, 2 + 2 * (it % 3))
-        forward(it // 3, 3 + 2 * (it % 3))
-        return 0
-
-    lax.fori_loop(0, GROUPS * 3, fwd_step, 0)
+            for n, (g, _) in enumerate(blocks):
+                z = scores[n][h * 128:(h + 1) * 128] * factor2 + bias[4 * g + h]
+                e = jnp.exp2(z - jnp.max(z, axis=0, keepdims=True))
+                probs[n].append((e * (1.0 / jnp.sum(e, axis=0, keepdims=True))).astype(BF16))
+        for n, (g, w) in enumerate(blocks):
+            stack = jnp.concatenate(probs[n], axis=0)
+            soft[g, w] = stack
+            rows = pl.ds(pl.multiple_of(g * 128, 128), 128)
+            att_t[rows, w * WIN:(w + 1) * WIN] = mm(head_rows(qkv[8 + g, w].T), stack).astype(BF16)
+
+    def fwd_step(g, _):
+        forward([(g, w) for w in range(2, NWIN)])
+        return 0
+
+    lax.fori_loop(0, GROUPS, fwd_step, 0)
 
     for copy in halo:
         copy.wait_recv()
@@ -370,12 +377,11 @@
     lax.fori_loop(0, 2, norm_win, 0)
     project(0, 0)
 
-    def fwd_late(g, _):
-        forward(g, 0)
-        forward(g, 1)
-        return 0
-
-    lax.fori_loop(0, GROUPS, fwd_late, 0)
+    def fwd_late(i, _):
+        forward([(2 * i + n, w) for n in range(2) for w in range(2)])
+        return 0
+
+    lax.fori_loop(0, GROUPS // 2, fwd_late, 0)
 
     def order_rows(m, _):
         cols = pl.ds(pl.multiple_of(m * 256, 256), 256)
@@ -394,31 +400,27 @@
 
     factor = HD ** (-0.5)
 
-    def backward(g, w):
-        q = qkv[g, w]
-        k = qkv[4 + g, w]
-        v = qkv[8 + g, w]
-        dhm = stack_heads(dh[g, w])
-        k_t = k.T
-        p_all = soft[g, w]
-        ds_t = mm(v, dhm, NT)
-        low = []
-        dq_t = []
+    def backward(g, windows):
+        grads = [mm(stack_heads(qkv[8 + g, w]), dh[g, w], NT) for w in windows]
+        low = [[] for _ in windows]
         for h in range(4):
             hs = slice(h * 128, (h + 1) * 128)
-            p = p_all[:, hs].astype(F32)
-            t = p * ds_t[:, hs]
-            dsc = t - p * jnp.sum(t, axis=0, keepdims=True)
-            dsum[:, hs] = dsum[:, hs] + dsc
-            lo = dsc.astype(BF16)
-            low.append(lo)
-            dq_t.append(mm(k_t[h * HD:(h + 1) * HD], lo))
-        dv = mm(p_all, dhm)
-        dk = mm(jnp.concatenate(low, axis=1), stack_heads(q)) * factor
-        dq = (jnp.concatenate(dq_t, axis=0) * factor).T
-        dproj[0, g, w] = dq.astype(BF16)
-        dproj[1, g, w] = dk.astype(BF16)
-        dproj[2, g, w] = dv.astype(BF16)
+            total = dsum[hs]
+            for n, w in enumerate(windows):
+                p = soft[g, w, hs].astype(F32)
+                t = p * grads[n][hs]
+                dsc = t - p * jnp.sum(t, axis=0, keepdims=True)
+                total = total + dsc
+                low[n].append(dsc.astype(BF16))
+            dsum[hs] = total
+        for n, w in enumerate(windows):
+            wide = jnp.concatenate([soft[g, w, h * 128:(h + 1) * 128] for h in range(4)], axis=1)
+            dv = mm(wide, stack_heads(dh[g, w]))
+            dk = mm(jnp.concatenate(low[n], axis=1), stack_heads(qkv[g, w])) * factor
+            dq = mm(head_rows(qkv[4 + g, w].T), jnp.concatenate(low[n], axis=0)) * factor
+            dproj[0, g, w] = dq.astype(BF16).T
+            dproj[1, g, w] = dk.astype(BF16)
+            dproj[2, g, w] = dv.astype(BF16)
 
     def store(p):
         total, table_sum = pieces[p].step4()
@@ -438,20 +440,18 @@
     for g in range(GROUPS):
         dsum[...] = jnp.zeros_like(dsum)
 
-        def bwd_step(i, _):
-            backward(g, 2 * i)
-            backward(g, 2 * i + 1)
-            if g >= 1:
-                pl.when(i == 0)(pieces[g - 1].step2)
-            if g >= 2:
-                pl.when(i == 0)(pieces[g - 2].step3)
-                pl.when(i == 3)(functools.partial(store, g - 2))
-            pl.when(i == 1)(pieces[g].step1)
-            return 0
-
-        lax.fori_loop(0, NWIN // 2, bwd_step, 0)
-
-        flipped = sum(mm(reverse, part) for part in split3(dsum[...]))
+        backward(g, range(0, 4))
+        if g >= 3:
+            store(g - 3)
+        if g >= 2:
+            pieces[g - 2].step3()
+        pieces[g].step1()
+        backward(g, range(4, 8))
+        if g >= 1:
+            pieces[g - 1].step2()
+
+        sums = jnp.concatenate([dsum[h * 128:(h + 1) * 128] for h in range(4)], axis=1)
+        flipped = sum(mm(reverse, part) for part in split3(sums))
         heads = bias_sums.setdefault(min(p for p in TABLE_GROUPS if g in TABLE_GROUPS[p]), [])
         for h in range(4):
             u = pltpu.roll(flipped[:, h * 128:(h + 1) * 128], 1, 1, stride=1, stride_axis=0)
@@ -489,15 +489,16 @@
     home = remote(ow.at[0], back_ref, halo_send.at[2], halo_recv.at[2], here.slab(-1))
     home.start()
     pieces[GROUPS - 2].step3()
-    pieces[GROUPS - 1].step2()
     last.step1()
     norm_grad(1, 0)
     norm_grad(2, 0)
-    pieces[GROUPS - 1].step3()
+    pieces[GROUPS - 1].step2()
     norm_grad(3, 0)
+    store(GROUPS - 3)
+    lax.fori_loop(1, NWIN, finish, 0)
     store(GROUPS - 2)
     last.step2()
-    lax.fori_loop(1, NWIN, finish, 0)
+    pieces[GROUPS - 1].step3()
 
     to_slab = one_hot(c_i == w_i + s)
     edge_slab = one_hot(t_c == t_w + s - 16)
@@ -508,10 +509,8 @@
         out_ref[r] = mm(to_slab, src).astype(BF16)
         return 0
 
-    last.step3()
     lax.fori_loop(0, WH, out_row, 0)
 
-    store(GROUPS - 1)
     home.wait_recv()
 
     def edge_row(r, _):
@@ -521,6 +520,8 @@
         return 0
 
     lax.fori_loop(0, WH, edge_row, 0)
+    last.step3()
+    store(GROUPS - 1)
 
     pick = iota((16, C), 1) == 2 * (here.lon * 4 + here.lat) + iota((16, C), 0)
     w_rows = mm(one_hot(pick), wqkv_ref[...])[0:2]
@@ -586,11 +587,11 @@
             pltpu.VMEM((C, TOK), BF16),
             pltpu.VMEM((12, NWIN, WIN, 128), BF16),
             pltpu.VMEM((GROUPS, NWIN, WIN, 128), BF16),
-            pltpu.VMEM((GROUPS, NWIN, WIN, 512), BF16),
+            pltpu.VMEM((GROUPS, NWIN, 512, WIN), BF16),
             pltpu.VMEM((C, TOK), BF16),
             pltpu.VMEM((3, GROUPS, NWIN, WIN, 128), BF16),
             pltpu.VMEM((NWIN, WIN, C), F32),
-            pltpu.VMEM((WIN, 512), F32),
+            pltpu.VMEM((512, WIN), F32),
             pltpu.VMEM((H, WIN, WIN), F32),
             pltpu.VMEM((512, 512), BF16),
             pltpu.VMEM((H, 512), F32),

time: 78.1 us -> 68.8 us (0.88)
  Pallas kernels: 76.7 us -> 67.3 us
    pallas_call x1, Pallas kernels: 74.5 us -> 65.1 us  [fused(): pl.pallas_call(functools.partial(body, n_dev), out_shape=(jax.ShapeDtypeS...]
where the time goes in v3:
time: 68.8 us; the launch traced here: 68.7 us
  Pallas kernels  67.3 us (98%)
  between operations  1.45 us (2%)
    pallas_call x1, Pallas kernels, fused(): pl.pallas_call(functools.partial(body, n_dev), out_shape=(jax.ShapeDtypeS...  65.1 us
    pallas_call x1, Pallas kernels, handover(): pl.pallas_call(functools.partial(handover_body, n), out_shape=tuple((jax....  2.19 us

profile of v3, /device:TPU:8, one launch (start us, length us, event | category | flops | bytes accessed | tf_op | source)
XLA Modules:
  0.0 68.7 jit_solution(2287621631919554495)
XLA Ops:
  1.3 65.1 %fused.1 = (bf16[8,128,512]{2,1,0:T(8,128)(2,1)}, f32[2,1536]{1,0:T(2,128)}, f32[2,512]{1,0:T(2,128)}, f32[1,2]{1,0:T(1,128)}, f32[16,465]{1,0:T(8,128)}) custom-call(s32[1]{0:T(128)S(6)} %copy.13.shift_ref, bf16[8,128,512]{2,1,0:T(8,128)(2,1)} %x_ref.1, bf16[8,128,512]{2,1,0:T(8,128)(2,1)} %d_ref.1, bf16[512,1536]{1,0:T(8,128)(2,1)} %wqkv_ref.1, ...), custom_call_target="tpu_custom_call" | custom-call | tf_op jit(solution)/shard_map/fused/pallas_call | solution.py:570
  66.4 2.2 %handover.1 = (bf16[8,128,512]{2,1,0:T(8,128)(2,1)}, f32[2,1536]{1,0:T(2,128)}, f32[2,512]{1,0:T(2,128)}, f32[1,2]{1,0:T(1,128)}, f32[16,465]{1,0:T(8,128)}) custom-call(bf16[8,128,512]{2,1,0:T(8,128)(2,1)} %get-tuple-element.15.refs_0_, f32[2,1536]{1,0:T(2,128)} %get-tuple-element.16.refs_1_, f32[2,512]{1,0:T(2,128)} %get-tuple-element.17.refs_2_, ...), custom_call_target="tpu_custom_call" | custom-call | tf_op jit(solution)/shard_map/handover/pallas_call | solution.py:638

commit v4 on v3

--- a/solution.py
+++ b/solution.py
@@ -215,10 +215,10 @@
 
 def body(
     n_dev,
-    shift_ref, x_ref, d_ref, wqkv_ref, wproj_ref, gain_ref, table_ref, rel_ref,
+    shift_ref, x_ref, d_ref, wqkv_hbm, wproj_hbm, gain_ref, table_ref, rel_ref,
     out_ref, gq_ref, gp_ref, gg_ref, gt_ref,
     xw, dw, nx, istd, normed, normed_t, qkv, dh, soft, att_t, dproj, dnorm, dsum, bias, hot, g4, ow, att_p,
-    tx_ref, td_ref, back_ref, halo_send, halo_recv, *rest,
+    tx_ref, td_ref, back_ref, halo_send, halo_recv, wqkv_ref, wproj_ref, weight_sem, *rest,
 ):
     here = Place()
     peers = [here.partner(), here.slab(1), here.slab(-1)]
@@ -237,6 +237,13 @@
             table = (rest[base:base + 4], rest[base + 4:base + 8], rest[base + 8:base + 12])
         pieces.append(Reduction(here, refs, table))
 
+    weights = [
+        pltpu.make_async_copy(src, dst, weight_sem.at[n])
+        for n, (src, dst) in enumerate(((wqkv_hbm, wqkv_ref), (wproj_hbm, wproj_ref)))
+    ]
+    for copy in weights:
+        copy.start()
+
     s = shift_ref[0]
     w_i = iota((128, 128), 0)
     c_i = iota((128, 128), 1)
@@ -247,15 +254,15 @@
     gain = gain_ref[...]
     grad_scale = (TOK * n_dev) ** (-0.5)
 
-    def shift_row(r, _):
-        rows = pl.ds(pl.multiple_of(r * WW, WW), WW)
+    def shift_row(r):
+        rows = pl.ds(r * WW, WW)
         for src, dst in ((x_ref, xw), (d_ref, dw)):
             y = mm(to_win, src[r]).astype(BF16)
             for w in range(NWIN):
                 dst[w, rows, :] = y[w * WW:(w + 1) * WW]
-        return 0
-
-    lax.fori_loop(0, WH, shift_row, 0)
+
+    for n in range(0, WH):
+        shift_row(n)
 
     pl.semaphore_wait(barrier, len(peers))
 
@@ -291,7 +298,7 @@
         )
         bias[h] = pltpu.roll(base, 0, 1, stride=1, stride_axis=0)
 
-    def norm_win(w, _):
+    def norm_win(w):
         src = xw[w].astype(F32)
         mean = jnp.mean(src, axis=-1, keepdims=True)
         cen = src - mean
@@ -300,9 +307,9 @@
         nx[w] = n
         istd[w] = inv
         normed[w] = (n * gain).astype(BF16)
-        return 0
-
-    lax.fori_loop(2, NWIN, norm_win, 0)
+
+    for n in range(2, NWIN):
+        norm_win(n)
 
     row_p = iota((C, C), 0)
     p_core, p_a, p_b = row_p // 256, (row_p // 64) % 4, (row_p // 16) % 4
@@ -312,7 +319,7 @@
     source = (p_x // 2) * 256 + p_z * 32 + p_y * 8 + (p_x % 2) * 4 + p_core * 2 + p_t
     order = one_hot(iota((C, C), 1) == source)
 
-    def project(m, _):
+    def project(m):
         lhs = normed[pl.ds(2 * m, 2)].reshape(256, C)
         for n in range(3):
             y = mm(lhs, wqkv_ref[:, n * C:(n + 1) * C]).astype(BF16)
@@ -323,10 +330,12 @@
         for b in range(4):
             for ww in range(2):
                 dh[b, 2 * m + ww] = y[ww * 128:(ww + 1) * 128, b * 128:(b + 1) * 128]
-        normed_t[:, pl.ds(pl.multiple_of(m * 256, 256), 256)] = mm(order, lhs, NT).astype(BF16)
-        return 0
-
-    lax.fori_loop(1, 4, project, 0)
+        normed_t[:, pl.ds(m * 256, 256)] = mm(order, lhs, NT).astype(BF16)
+
+    for copy in weights:
+        copy.wait()
+    for n in range(1, 4):
+        project(n)
     masks = head_masks(128)
 
     def stack_heads(block):
@@ -366,16 +375,17 @@
     for copy in halo:
         copy.wait_recv()
 
-    def tail_row(r, _):
-        rows = pl.ds(pl.multiple_of(r * WW, WW), WW)
+    def tail_row(r):
+        rows = pl.ds(r * WW, WW)
         for src, dst in ((tx_ref, xw), (td_ref, dw)):
             y = mm(tail_win, src[r]).astype(BF16)
             dst[0, rows, :] = dst[0, rows, :] + y
-        return 0
-
-    lax.fori_loop(0, WH, tail_row, 0)
-    lax.fori_loop(0, 2, norm_win, 0)
-    project(0, 0)
+
+    for n in range(0, WH):
+        tail_row(n)
+    for n in range(0, 2):
+        norm_win(n)
+    project(0)
 
     def fwd_late(i, _):
         forward([(2 * i + n, w) for n in range(2) for w in range(2)])
@@ -383,20 +393,23 @@
 
     lax.fori_loop(0, GROUPS // 2, fwd_late, 0)
 
-    def order_rows(m, _):
-        cols = pl.ds(pl.multiple_of(m * 256, 256), 256)
+    def order_rows(m):
+        cols = pl.ds(m * 256, 256)
         att_p[:, cols] = mm(order, att_t[:, cols]).astype(BF16)
-        return 0
-
-    lax.fori_loop(0, 4, order_rows, 0)
-
-    def to_send(piece, y):
-        y = (y * grad_scale).astype(BF16)
-        for n in range(32):
-            piece.s0[n // 16, (n // 4) % 4, n % 4] = y[n * 16:(n + 1) * 16]
-
-    to_send(pieces[0], mm(att_p[...], dw[...].reshape(TOK, C)))
-    pieces[0].start()
+
+    for n in range(0, 4):
+        order_rows(n)
+
+    def to_send(piece, rows_ref, other, table_value=None):
+        for core in (1 - here.core, here.core):
+            rows = pl.ds(pl.multiple_of(core * 256, 256), 256)
+            y = (mm(rows_ref[rows, :], other) * grad_scale).astype(BF16)
+            for n in range(16):
+                piece.s0[core, n // 4, n % 4] = y[n * 16:(n + 1) * 16]
+            if core is not here.core:
+                piece.start(table_value)
+
+    to_send(pieces[0], att_p, dw[...].reshape(TOK, C))
 
     factor = HD ** (-0.5)
 
@@ -441,14 +454,13 @@
         dsum[...] = jnp.zeros_like(dsum)
 
         backward(g, range(0, 4))
-        if g >= 3:
-            store(g - 3)
-        if g >= 2:
-            pieces[g - 2].step3()
+        if g == 2:
+            pieces[0].step2()
+        if g == 3:
+            pieces[1].step2()
+            pieces[0].step3()
+        backward(g, range(4, 8))
         pieces[g].step1()
-        backward(g, range(4, 8))
-        if g >= 1:
-            pieces[g - 1].step2()
 
         sums = jnp.concatenate([dsum[h * 128:(h + 1) * 128] for h in range(4)], axis=1)
         flipped = sum(mm(reverse, part) for part in split3(sums))
@@ -460,68 +472,70 @@
                 heads.append(jnp.sum(jnp.where(keep, u, 0.0), axis=0, keepdims=True))
 
         grads = jnp.concatenate([dproj[b, g].reshape(TOK, 128) for b in range(3)], axis=1)
-        to_send(pieces[g + 1], mm(normed_t[...], grads))
-        pieces[g + 1].start(
-            jnp.concatenate(bias_sums[g + 1], axis=0) if g + 1 in TABLE_GROUPS else None
+        to_send(
+            pieces[g + 1], normed_t, grads,
+            jnp.concatenate(bias_sums[g + 1], axis=0) if g + 1 in TABLE_GROUPS else None,
         )
 
-    def norm_grad(m, _):
+    def norm_grad(m):
         lhs = jnp.concatenate(
             [dproj[b, g, pl.ds(2 * m, 2)].reshape(256, 128) for b in range(3) for g in range(GROUPS)],
             axis=1,
         )
         dnorm[pl.ds(2 * m, 2)] = mm(lhs, wqkv_ref[...], NT).reshape(2, WIN, C)
-        return 0
 
     last = pieces[GROUPS]
 
-    def finish(w, _):
+    def finish(w):
         n = nx[w]
         sc = dnorm[w] * gain
         m1 = jnp.mean(sc, axis=-1, keepdims=True)
         m2 = jnp.mean(sc * n, axis=-1, keepdims=True)
         branch = istd[w] * (sc - m1 - n * m2)
         ow[w] = (dw[w].astype(F32) + branch).astype(BF16)
-        return 0
-
-    norm_grad(0, 0)
-    finish(0, 0)
+
+    norm_grad(0)
+    finish(0)
     home = remote(ow.at[0], back_ref, halo_send.at[2], halo_recv.at[2], here.slab(-1))
     home.start()
-    pieces[GROUPS - 2].step3()
+    pieces[2].step2()
     last.step1()
-    norm_grad(1, 0)
-    norm_grad(2, 0)
-    pieces[GROUPS - 1].step2()
-    norm_grad(3, 0)
-    store(GROUPS - 3)
-    lax.fori_loop(1, NWIN, finish, 0)
-    store(GROUPS - 2)
-    last.step2()
-    pieces[GROUPS - 1].step3()
+    norm_grad(1)
+    norm_grad(2)
+    pieces[1].step3()
+    store(0)
+    norm_grad(3)
+    for n in range(1, NWIN):
+        finish(n)
+    pieces[3].step2()
+    pieces[2].step3()
 
     to_slab = one_hot(c_i == w_i + s)
     edge_slab = one_hot(t_c == t_w + s - 16)
 
-    def out_row(r, _):
-        rows = pl.ds(pl.multiple_of(r * WW, WW), WW)
+    def out_row(r):
+        rows = pl.ds(r * WW, WW)
         src = jnp.concatenate([ow[w, rows, :] for w in range(NWIN)], axis=0)
         out_ref[r] = mm(to_slab, src).astype(BF16)
-        return 0
-
-    lax.fori_loop(0, WH, out_row, 0)
+
+    for n in range(0, WH):
+        out_row(n)
 
     home.wait_recv()
 
-    def edge_row(r, _):
-        rows = pl.ds(pl.multiple_of(r * WW, WW), WW)
+    def edge_row(r):
+        rows = pl.ds(r * WW, WW)
         y = mm(edge_slab, back_ref[rows, :]).astype(BF16)
         out_ref[r, COLS - WW:, :] = out_ref[r, COLS - WW:, :] + y
-        return 0
-
-    lax.fori_loop(0, WH, edge_row, 0)
+
+    for n in range(0, WH):
+        edge_row(n)
+    last.step2()
+    store(1)
+    pieces[3].step3()
+    store(2)
     last.step3()
-    store(GROUPS - 1)
+    store(3)
 
     pick = iota((16, C), 1) == 2 * (here.lon * 4 + here.lat) + iota((16, C), 0)
     w_rows = mm(one_hot(pick), wqkv_ref[...])[0:2]
@@ -567,6 +581,7 @@
 
 def fused(n_dev, *args):
     vm = pl.BlockSpec(memory_space=pltpu.VMEM)
+    hbm = pl.BlockSpec(memory_space=pl.ANY)
     return pl.pallas_call(
         functools.partial(body, n_dev),
         out_shape=(
@@ -576,7 +591,7 @@
             jax.ShapeDtypeStruct((1, 2), F32),
             jax.ShapeDtypeStruct((H, NREL), F32),
         ),
-        in_specs=[pl.BlockSpec(memory_space=pltpu.SMEM)] + [vm] * 7,
+        in_specs=[pl.BlockSpec(memory_space=pltpu.SMEM), vm, vm, hbm, hbm, vm, vm, vm],
         out_specs=(vm,) * 5,
         scratch_shapes=[
             pltpu.VMEM((NWIN, WIN, C), BF16),
@@ -602,6 +617,9 @@
             pltpu.VMEM((WIN, C), BF16),
             pltpu.SemaphoreType.DMA((3,)),
             pltpu.SemaphoreType.DMA((3,)),
+            pltpu.VMEM((C, 3 * C), BF16),
+            pltpu.VMEM((C, C), BF16),
+            pltpu.SemaphoreType.DMA((2,)),
         ]
         + [ref for width in PIECES for ref in piece_scratch(width)]
         + [ref for groups in TABLE_GROUPS.values() for ref in table_scratch(len(groups))],

time: 68.8 us -> 59 us (0.86)
  Pallas kernels: 67.3 us -> 57.4 us
    pallas_call x1, Pallas kernels: 65.1 us -> 55.2 us  [fused(): pl.pallas_call(functools.partial(body, n_dev), out_shape=(jax.ShapeDtypeS...]
where the time goes in v4:
time: 59 us; the launch traced here: 58.8 us
  Pallas kernels  57.4 us (97%)
  between operations  1.47 us (2%)
    pallas_call x1, Pallas kernels, fused(): pl.pallas_call(functools.partial(body, n_dev), out_shape=(jax.ShapeDtypeS...  55.2 us
    pallas_call x1, Pallas kernels, handover(): pl.pallas_call(functools.partial(handover_body, n), out_shape=tuple((jax....  2.19 us

profile of v4, /device:TPU:8, one launch (start us, length us, event | category | flops | bytes accessed | tf_op | source)
XLA Modules:
  0.0 58.8 jit_solution(11515492331130125599)
XLA Ops:
  1.3 55.2 %fused.1 = (bf16[8,128,512]{2,1,0:T(8,128)(2,1)}, f32[2,1536]{1,0:T(2,128)}, f32[2,512]{1,0:T(2,128)}, f32[1,2]{1,0:T(1,128)}, f32[16,465]{1,0:T(8,128)}) custom-call(s32[1]{0:T(128)S(6)} %copy.13.shift_ref, bf16[8,128,512]{2,1,0:T(8,128)(2,1)} %x_ref.1, bf16[8,128,512]{2,1,0:T(8,128)(2,1)} %d_ref.1, bf16[512,1536]{1,0:T(8,128)(2,1)} %wqkv_hbm.1, ...), custom_call_target="tpu_custom_call" | custom-call | tf_op jit(solution)/shard_map/fused/pallas_call | solution.py:585
  56.5 2.2 %handover.1 = (bf16[8,128,512]{2,1,0:T(8,128)(2,1)}, f32[2,1536]{1,0:T(2,128)}, f32[2,512]{1,0:T(2,128)}, f32[1,2]{1,0:T(1,128)}, f32[16,465]{1,0:T(8,128)}) custom-call(bf16[8,128,512]{2,1,0:T(8,128)(2,1)} %get-tuple-element.15.refs_0_, f32[2,1536]{1,0:T(2,128)} %get-tuple-element.16.refs_1_, f32[2,512]{1,0:T(2,128)} %get-tuple-element.17.refs_2_, ...), custom_call_target="tpu_custom_call" | custom-call | tf_op jit(solution)/shard_map/handover/pallas_call | solution.py:656

commit v5 on v4

--- a/solution.py
+++ b/solution.py
@@ -60,8 +60,8 @@
 
 
 NX, NY, NZ = 4, 4, 8
-PIECES = (C, 384, 384, 384, 384)
-TABLE_GROUPS = {3: (0, 1, 2), 4: (3,)}
+PIECES = (C, 768, 768)
+TABLE_GROUPS = {1: (0, 1), 2: (2, 3)}
 
 
 class Place:
@@ -440,8 +440,10 @@
         if p == 0:
             gp_ref[...] = total
         else:
-            for b in range(3):
-                gq_ref[:, b * C + (p - 1) * 128:b * C + p * 128] = total[:, b * 128:(b + 1) * 128]
+            for n, group in enumerate(TABLE_GROUPS[p]):
+                for b in range(3):
+                    k = (3 * n + b) * 128
+                    gq_ref[:, b * C + group * 128:b * C + (group + 1) * 128] = total[:, k:k + 128]
         if p in TABLE_GROUPS:
             for n, group in enumerate(TABLE_GROUPS[p]):
                 for h in range(4):
@@ -456,11 +458,13 @@
         backward(g, range(0, 4))
         if g == 2:
             pieces[0].step2()
+        backward(g, range(4, 8))
+        if g == 0:
+            pieces[0].step1()
+        if g == 2:
+            pieces[1].step1()
         if g == 3:
-            pieces[1].step2()
             pieces[0].step3()
-        backward(g, range(4, 8))
-        pieces[g].step1()
 
         sums = jnp.concatenate([dsum[h * 128:(h + 1) * 128] for h in range(4)], axis=1)
         flipped = sum(mm(reverse, part) for part in split3(sums))
@@ -471,11 +475,12 @@
                 keep = (wrap_r if q // 2 else ~wrap_r) & (carry_r if q % 2 else ~carry_r)
                 heads.append(jnp.sum(jnp.where(keep, u, 0.0), axis=0, keepdims=True))
 
-        grads = jnp.concatenate([dproj[b, g].reshape(TOK, 128) for b in range(3)], axis=1)
-        to_send(
-            pieces[g + 1], normed_t, grads,
-            jnp.concatenate(bias_sums[g + 1], axis=0) if g + 1 in TABLE_GROUPS else None,
-        )
+        if g % 2:
+            piece = (g + 1) // 2
+            grads = jnp.concatenate(
+                [dproj[b, k].reshape(TOK, 128) for k in (g - 1, g) for b in range(3)], axis=1
+            )
+            to_send(pieces[piece], normed_t, grads, jnp.concatenate(bias_sums[piece], axis=0))
 
     def norm_grad(m):
         lhs = jnp.concatenate(
@@ -484,7 +489,7 @@
         )
         dnorm[pl.ds(2 * m, 2)] = mm(lhs, wqkv_ref[...], NT).reshape(2, WIN, C)
 
-    last = pieces[GROUPS]
+    last = pieces[2]
 
     def finish(w):
         n = nx[w]
@@ -498,17 +503,15 @@
     finish(0)
     home = remote(ow.at[0], back_ref, halo_send.at[2], halo_recv.at[2], here.slab(-1))
     home.start()
-    pieces[2].step2()
     last.step1()
     norm_grad(1)
+    pieces[1].step2()
     norm_grad(2)
-    pieces[1].step3()
+    norm_grad(3)
     store(0)
-    norm_grad(3)
     for n in range(1, NWIN):
         finish(n)
-    pieces[3].step2()
-    pieces[2].step3()
+    pieces[1].step3()
 
     to_slab = one_hot(c_i == w_i + s)
     edge_slab = one_hot(t_c == t_w + s - 16)
@@ -532,16 +535,13 @@
         edge_row(n)
     last.step2()
     store(1)
-    pieces[3].step3()
-    store(2)
     last.step3()
-    store(3)
 
     pick = iota((16, C), 1) == 2 * (here.lon * 4 + here.lat) + iota((16, C), 0)
     w_rows = mm(one_hot(pick), wqkv_ref[...])[0:2]
     gain_rows = jnp.sum(jnp.where(pick, jnp.broadcast_to(gain, (16, C)), 0.0), axis=1, keepdims=True)[0:2]
 
-    store(GROUPS)
+    store(2)
     gg = jnp.sum(gq_ref[...] * w_rows, axis=1, keepdims=True) / gain_rows
     gg_ref[...] = jnp.where(iota((1, 2), 1) == 0, gg[0:1], gg[1:2])
 

time: 59 us -> 60.6 us (1.027)
  Pallas kernels: 57.4 us -> 59 us
    pallas_call x1, Pallas kernels: 55.2 us -> 56.8 us  [fused(): pl.pallas_call(functools.partial(body, n_dev), out_shape=(jax.ShapeDtypeS...]
where the time goes in v5:
time: 60.6 us; the launch traced here: 60.5 us
  Pallas kernels  59 us (97%)
  between operations  1.45 us (2%)
    pallas_call x1, Pallas kernels, fused(): pl.pallas_call(functools.partial(body, n_dev), out_shape=(jax.ShapeDtypeS...  56.8 us
    pallas_call x1, Pallas kernels, handover(): pl.pallas_call(functools.partial(handover_body, n), out_shape=tuple((jax....  2.19 us

profile of v5, /device:TPU:8, one launch (start us, length us, event | category | flops | bytes accessed | tf_op | source)
XLA Modules:
  0.0 60.5 jit_solution(17705027782626774954)
XLA Ops:
  1.3 56.8 %fused.1 = (bf16[8,128,512]{2,1,0:T(8,128)(2,1)}, f32[2,1536]{1,0:T(2,128)}, f32[2,512]{1,0:T(2,128)}, f32[1,2]{1,0:T(1,128)}, f32[16,465]{1,0:T(8,128)}) custom-call(s32[1]{0:T(128)S(6)} %copy.13.shift_ref, bf16[8,128,512]{2,1,0:T(8,128)(2,1)} %x_ref.1, bf16[8,128,512]{2,1,0:T(8,128)(2,1)} %d_ref.1, bf16[512,1536]{1,0:T(8,128)(2,1)} %wqkv_hbm.1, ...), custom_call_target="tpu_custom_call" | custom-call | tf_op jit(solution)/shard_map/fused/pallas_call | solution.py:585
  58.1 2.2 %handover.1 = (bf16[8,128,512]{2,1,0:T(8,128)(2,1)}, f32[2,1536]{1,0:T(2,128)}, f32[2,512]{1,0:T(2,128)}, f32[1,2]{1,0:T(1,128)}, f32[16,465]{1,0:T(8,128)}) custom-call(bf16[8,128,512]{2,1,0:T(8,128)(2,1)} %get-tuple-element.15.refs_0_, f32[2,1536]{1,0:T(2,128)} %get-tuple-element.16.refs_1_, f32[2,512]{1,0:T(2,128)} %get-tuple-element.17.refs_2_, ...), custom_call_target="tpu_custom_call" | custom-call | tf_op jit(solution)/shard_map/handover/pallas_call | solution.py:656
